TPU v7x, 32 devices: a whole 2x2x4 slice. The times are simulated.
32 devices in a mesh: row: 8 (over z, core), col: 4 (over y, x).
Axes of the slice: x: 2, y: 2, z: 4, core: 2. Of those that a mesh axis runs over, the one named last changes fastest.
Arguments:
- base_weight: bfloat16 [16384, 49152], P('row', 'col'), may hold values from -6 to 6
- left_factor: float32 [16384, 256], P('row', 'col'), may hold values from -6 to 6
- right_factor: float32 [256, 49152], P('row', 'col'), may hold values from -0.375 to 0.375
Outputs:
- merged: bfloat16 [16384, 49152], P(None, ('row', 'col'))
All inputs are finite; a program needn't handle non-finite values.
Results may differ from a plain program's by a relative error of at most 0.001.
Values may be sent and summed in bfloat16 or wider, within the bound.
A program may use at most 256 MiB of HBM per device.

v0:
```python
import jax
import jax.numpy as jnp
from jax import lax
from jax.sharding import PartitionSpec as P


def to_serving(stored):
    row_count = lax.axis_size("row")
    col_count = lax.axis_size("col")
    height = stored.shape[0]
    block_width = stored.shape[1] // row_count
    group_count = row_count // col_count
    shaped = stored.reshape(height, group_count, col_count, block_width)
    across = lax.all_to_all(shaped, "col", split_axis=2, concat_axis=1, tiled=True)
    served = lax.all_to_all(across, "row", split_axis=1, concat_axis=0, tiled=True)
    return served.reshape(height * row_count, block_width)


def body(base_weight, left_factor, right_factor):
    left_cols = lax.all_gather(left_factor, "col", axis=1, tiled=True)
    delta = jnp.dot(
        left_cols,
        lax.all_gather(right_factor, "row", axis=0, tiled=True),
        precision=lax.Precision.HIGHEST,
        preferred_element_type=jnp.float32,
    )
    merged_block = (base_weight.astype(jnp.float32) + delta).astype(jnp.bfloat16)
    return to_serving(merged_block)


def solution(mesh):
    placed = (P("row", "col"), P("row", "col"), P("row", "col"))
    return jax.shard_map(
        body, mesh=mesh, in_specs=placed, out_specs=P(None, ("row", "col")), check_vma=False
    )
```

profile of v0, /device:TPU:5, one launch (start us, length us, event | category | flops | bytes accessed | tf_op | source)
XLA Modules:
  0.0 2062.7 jit_solution(7869436619697725776)
XLA Ops:
  6.5 0.0 all-gather.3.cloned.1.call-start
  6.5 0.7 all-gather.3.cloned.1.call-update
  7.3 0.0 all-gather.5.cloned.1.call-start
  7.3 0.7 all-gather.5.cloned.1.call-update
  8.0 37.4 %all-gather.3.cloned.1.call-done = f32[2048,256]{0,1:T(8,128)} async-done(((f32[2048,64]{0,1:T(8,128)}), f32[2048,256]{0,1:T(8,128)}) %all-gather.3.cloned.1.call-update) | async-done | bytes 2097168 | tf_op jit(solution)/shard_map/all_gather | solution.py:20
  45.4 119.0 %all-gather.5.cloned.1.call-done = f32[256,12288]{1,0:T(8,128)} async-done(((f32[32,12288]{1,0:T(8,128)}), f32[256,12288]{1,0:T(8,128)}) %all-gather.5.cloned.1.call-update) | async-done | bytes 12582928 | tf_op jit(solution)/shard_map/all_gather | solution.py:23
  164.4 90.8 %add_convert_fusion = bf16[2048,12288]{1,0:T(8,128)(2,1)} fusion(bf16[2048,12288]{1,0:T(8,128)(2,1)} %param.3, f32[2048,256]{0,1:T(8,128)} %all-gather.3.cloned.1.call-done, f32[256,12288]{1,0:T(8,128)} %all-gather.5.cloned.1.call-done), kind=kOutput, calls=%fused_computation | convolution fusion | flops 77384908800 | bytes 115343360 | tf_op jit(solution)/shard_map/dot_general | solution.py:21
  255.1 96.7 %reshape.7 = bf16[2048,2,4,1536]{3,2,1,0:T(4,128)(2,1)} reshape(bf16[2048,12288]{1,0:T(8,128)(2,1)} %add_convert_fusion) | data formatting | bytes 100663296 | tf_op jit(solution)/shard_map/reshape | solution.py:13
  351.8 33.9 %copy.5 = bf16[2048,2,4,1536]{3,0,1,2:T(8,128)(2,1)} copy(bf16[2048,2,4,1536]{3,2,1,0:T(4,128)(2,1)} %reshape.7) | data formatting | bytes 100663296 | tf_op jit(solution)/shard_map/reshape | solution.py:13
  385.7 548.6 %all_to_all.33 = bf16[2048,2,4,1536]{3,0,1,2:T(8,128)(2,1)S(1)} all-to-all(bf16[2048,2,4,1536]{3,0,1,2:T(8,128)(2,1)} %copy.5), channel_id=1, replica_groups=mesh['row'=8,'col'=4] {'col'}, dimensions={2} | all-to-all | bytes 100663296 | tf_op jit(solution)/shard_map/all_to_all | solution.py:14
  934.3 1087.9 %all_to_all.34 = bf16[2048,8,1,1536]{3,0,2,1:T(8,128)(2,1)} all-to-all(bf16[2048,8,1,1536]{3,0,2,1:T(8,128)(2,1)S(1)} %bitcast.14), channel_id=1, replica_groups=mesh['row'=8,'col'=4] {'row'}, dimensions={1} | all-to-all | bytes 100663296 | tf_op jit(solution)/shard_map/all_to_all | solution.py:15
  2022.2 33.7 %copy.8 = bf16[16384,1536]{1,0:T(8,128)(2,1)} copy(bf16[16384,1536]{1,0:T(8,128)(2,1)} %bitcast.15) | data formatting | bytes 100663296
Async XLA Ops:
  6.5 38.9 %all-gather.3.cloned.1.call-start = ((), (), s32[]{:S(2)}) async-start(), calls=%async_computation.2 | async-start | bytes 2621440 | tf_op jit(solution)/shard_map/all_gather | solution.py:20
  7.3 157.1 %all-gather.5.cloned.1.call-start = ((), (), s32[]{:S(2)}) async-start(), calls=%async_computation.3 | async-start | bytes 14155776 | tf_op jit(solution)/shard_map/all_gather | solution.py:23
Sparse Core Ops, SparseCore 0:
  9.2 36.1 all-gather.2
  47.1 117.2 all-gather.4
where the time goes:
time: 2070 us; the launch traced here: 2060 us
  blocking collectives  1640 us (79%)
  local copies, waits for them, and re-layouts  164 us (8%)
  waiting for transfers between devices  158 us (8%)
  matrix products  90.8 us (4%)
    all_to_all x1, blocking collectives, to_serving(): lax.all_to_all(across, 'row', split_axis=1, concat_axis=0, tiled=True)  1090 us
    all_to_all x1, blocking collectives, to_serving(): lax.all_to_all(shaped, 'col', split_axis=2, concat_axis=1, tiled=True)  549 us
    reshape x2, local copies, waits for them, and re-layouts, to_serving(): shaped = stored.reshape(height, group_count, col_count, block_width)  131 us
    all_gather x1, waiting for transfers between devices, body(): lax.all_gather(right_factor, 'row', axis=0, tiled=True)  119 us
    dot_general x1, matrix products, body(): jnp.dot(left_cols, lax.all_gather(right_factor, 'row', axis=0, tiled=True...  90.8 us
  transfers between devices with their start and end apart: 2, of which 2 were waited for; matrix products, arithmetic and copies ran while one was open for 0% of the time, Pallas kernels for 0%

commit v1 on v0

v1 whole, which is shorter than its diff:
```python
import functools

import jax
import jax.numpy as jnp
from jax import lax
from jax.experimental import pallas as pl
from jax.experimental.pallas import tpu as pltpu
from jax.sharding import PartitionSpec as P

CHUNKS = 8
AHEAD = 2
MESH = pl.DeviceIdType.MESH


def transport(nr, nc, base, left, right, served, left_all, right_all, mid, mid_right, *sems):
    (a_send, a_recv, b_send, b_recv, ra_send, ra_recv, rb_send, rb_recv,
     l1_send, l1_recv, l2_send, l2_recv, l3_send, l3_recv, own_sem) = sems
    ng = nr // nc
    half = nr // 2
    height = base.shape[0]
    width = base.shape[1] // nr
    depth = right.shape[0]
    rank, left_width = left.shape
    step = height // CHUNKS
    r = lax.axis_index("row")
    c = lax.axis_index("col")
    sibling = r + 1 - 2 * lax.rem(r, 2)

    def remote(src, dst, send, recv, row, col):
        return pltpu.make_async_remote_copy(
            src_ref=src, dst_ref=dst, send_sem=send, recv_sem=recv, device_id=(row, col), device_id_type=MESH
        )

    def shifted(value, by, size):
        return lax.rem(value + by + size, size)

    def across(k, dj, g, src, final, middle, rows, send, recv, act):
        j = shifted(c, dj, nc)
        here = c * ng + g == r
        at = pl.ds(pl.multiple_of(k * rows, 8), rows)
        source = src.at[at, pl.ds(pl.multiple_of((g * nc + j) * width, 128), width)]
        sem = (k, dj - 1, g)

        @pl.when(here)
        def _():
            to = final.at[pl.ds(pl.multiple_of(r * src.shape[0] + k * rows, 8), rows), :]
            act(remote(source, to, send.at[sem], recv.at[sem], r, j))

        @pl.when(jnp.logical_not(here))
        def _():
            to = middle.at[c, g, at, :]
            act(remote(source, to, send.at[sem], recv.at[sem], r, j))

    def start(copy):
        copy.start()

    def wait_send(copy):
        copy.wait_send()

    def arrived(k, ds, g, src, final, middle, rows, send, recv):
        at = pl.ds(pl.multiple_of(k * rows, 8), rows)
        s = shifted(c, -ds, nc)
        here = s * ng + g == r
        sem = (k, ds - 1, g)

        @pl.when(here)
        def _():
            to = final.at[pl.ds(pl.multiple_of(r * src.shape[0] + k * rows, 8), rows), :]
            remote(to, to, send.at[sem], recv.at[sem], r, s).wait_recv()

        @pl.when(jnp.logical_not(here))
        def _():
            to = middle.at[s, g, at, :]
            remote(to, to, send.at[sem], recv.at[sem], r, s).wait_recv()

    def along(k, ds, g, src, final, middle, rows, send, recv, own, act, act_own):
        at = pl.ds(pl.multiple_of(k * rows, 8), rows)
        s = shifted(c, -ds, nc)
        to_row = s * ng + g
        if ds == 0:
            source = src.at[at, pl.ds(pl.multiple_of((g * nc + c) * width, 128), width)]
        else:
            source = middle.at[s, g, at, :]
        to = final.at[pl.ds(pl.multiple_of(r * src.shape[0] + k * rows, 8), rows), :]

        @pl.when(to_row != r)
        def _():
            act(remote(source, to, send.at[k, ds, g], recv.at[k, r], to_row, c))

        if ds == 0:
            @pl.when(to_row == r)
            def _():
                act_own(pltpu.make_async_copy(source, to, own.at[k]))

    def received(k, dq, final, rows, total, send, recv):
        q = shifted(r, -dq, nr)
        to = final.at[pl.ds(pl.multiple_of(q * total + k * rows, 8), rows), :]
        remote(to, to, send.at[k, 0, 0], recv.at[k, q], q, c).wait_recv()

    big = (base, served, mid, step)
    small = (right, right_all, mid_right, depth)
    own_big = own_sem.at[pl.ds(0, CHUNKS)]
    own_small = own_sem.at[pl.ds(CHUNKS, 1)]

    def each_across(k, arrays, send, recv, act):
        for g in range(ng):
            for dj in range(1, nc):
                across(k, dj, g, *arrays, send, recv, act)

    def each_along(k, shifts, arrays, send, recv, own, act, act_own):
        for ds in shifts:
            for g in range(ng):
                along(k, ds, g, *arrays, send, recv, own, act, act_own)

    def block(s, q):
        return left_all.at[
            pl.ds(pl.multiple_of(s * rank, 8), rank), pl.ds(pl.multiple_of(q * left_width, 128), left_width)
        ]

    def first_left(d):
        return remote(left, block(c, r), l1_send.at[d - 1], l1_recv.at[d - 1], shifted(r, 2 * d, nr), c)

    def second_left(d, dj):
        q = shifted(r, -2 * d, nr)
        source = left if d == 0 else block(c, q)
        return remote(source, block(c, q), l2_send.at[d, dj - 1], l2_recv.at[d, dj - 1], r, shifted(c, dj, nc))

    def third_left(d, ds):
        q = shifted(r, -2 * d, nr)
        s = shifted(c, -ds, nc)
        source = left if d == 0 and ds == 0 else block(s, q)
        return remote(source, block(s, q), l3_send.at[d, ds], l3_recv.at[d, ds], sibling, c)

    def got(sems_send, sems_recv, s, q):
        remote(block(s, q), block(s, q), sems_send, sems_recv, r, shifted(c, 1, nc)).wait_recv()

    barrier = pltpu.get_barrier_semaphore()
    for dj in range(1, nc):
        pl.semaphore_signal(barrier, inc=1, device_id=(r, shifted(c, dj, nc)), device_id_type=MESH)
    for dq in range(1, nr):
        pl.semaphore_signal(barrier, inc=1, device_id=(shifted(r, dq, nr), c), device_id_type=MESH)
    pl.semaphore_wait(barrier, nc + nr - 2)

    def open_chunk(k):
        each_across(k, big, a_send, a_recv, start)
        each_along(k, (0,), big, b_send, b_recv, own_big, start, start)

    each_across(0, big, a_send, a_recv, start)
    for d in range(1, half):
        first_left(d).start()
    each_along(0, (0,), big, b_send, b_recv, own_big, start, start)
    each_across(0, small, ra_send, ra_recv, start)
    each_along(0, (0,), small, rb_send, rb_recv, own_small, start, start)
    own_left = pltpu.make_async_copy(left, block(c, r), own_sem.at[CHUNKS + 1])
    own_left.start()

    @pl.loop(1, AHEAD)
    def _(k):
        open_chunk(k)

    def forward(k):
        for g in range(ng):
            for ds in range(1, nc):
                arrived(k, ds, g, *big, a_send, a_recv)
        each_along(k, range(1, nc), big, b_send, b_recv, own_big, start, start)

    @pl.loop(0, CHUNKS)
    def _(k):
        @pl.when(k + AHEAD < CHUNKS)
        def _():
            open_chunk(k + AHEAD)

        forward(k)

        @pl.when(k == 0)
        def _():
            for g in range(ng):
                for ds in range(1, nc):
                    arrived(0, ds, g, *small, ra_send, ra_recv)
            each_along(0, range(1, nc), small, rb_send, rb_recv, own_small, start, start)

    for d in range(half):
        if d > 0:
            got(l1_send.at[d - 1], l1_recv.at[d - 1], c, shifted(r, -2 * d, nr))
        for dj in range(1, nc):
            second_left(d, dj).start()
        third_left(d, 0).start()
    for d in range(half):
        for ds in range(1, nc):
            got(l2_send.at[d, ds - 1], l2_recv.at[d, ds - 1], shifted(c, -ds, nc), shifted(r, -2 * d, nr))
            third_left(d, ds).start()
    for d in range(half):
        for ds in range(nc):
            got(l3_send.at[d, ds], l3_recv.at[d, ds], shifted(c, -ds, nc), shifted(sibling, -2 * d, nr))
            third_left(d, ds).wait_send()
        for dj in range(1, nc):
            second_left(d, dj).wait_send()
        if d > 0:
            first_left(d).wait_send()
    own_left.wait()

    def finish(copy):
        copy.wait()

    def drain(k, arrays, a, b_s, b_r, own):
        each_across(k, arrays, *a, wait_send)
        each_along(k, range(nc), arrays, b_s, b_r, own, wait_send, finish)
        for dq in range(1, nr):
            received(k, dq, arrays[1], arrays[3], arrays[0].shape[0], b_s, b_r)

    drain(0, small, (ra_send, ra_recv), rb_send, rb_recv, own_small)

    @pl.loop(0, CHUNKS)
    def _(k):
        drain(k, big, (a_send, a_recv), b_send, b_recv, own_big)


def move(base_weight, left_turned, right_factor):
    nr = lax.axis_size("row")
    nc = lax.axis_size("col")
    ng = nr // nc
    half = nr // 2
    height, stored_width = base_weight.shape
    width = stored_width // nr
    depth = right_factor.shape[0]
    rank, left_width = left_turned.shape
    out = jax.ShapeDtypeStruct
    dma = pltpu.SemaphoreType.DMA
    anywhere = pl.BlockSpec(memory_space=pl.ANY)

    def stage_sems(chunks):
        a = (chunks, nc - 1, ng)
        return [dma(a), dma(a), dma((chunks, nc, ng)), dma((chunks, nr))]

    return pl.pallas_call(
        functools.partial(transport, nr, nc),
        out_shape=[
            out((nr * height, width), base_weight.dtype),
            out((nc * rank, nr * left_width), left_turned.dtype),
            out((nr * depth, width), right_factor.dtype),
            out((nc, ng, height, width), base_weight.dtype),
            out((nc, ng, depth, width), right_factor.dtype),
        ],
        in_specs=[anywhere] * 3,
        out_specs=[anywhere] * 5,
        scratch_shapes=[
            *stage_sems(CHUNKS),
            *stage_sems(1),
            dma((half - 1,)), dma((half - 1,)),
            dma((half, nc - 1)), dma((half, nc - 1)),
            dma((half, nc)), dma((half, nc)),
            dma((CHUNKS + 2,)),
        ],
        compiler_params=pltpu.CompilerParams(collective_id=0, has_side_effects=True),
    )(base_weight, left_turned, right_factor)


def body(base_weight, left_factor, right_factor):
    served, left_all, right_all, _, _ = move(base_weight, left_factor.T, right_factor)
    delta = lax.dot_general(
        left_all, right_all, (((0,), (0,)), ((), ())),
        precision=lax.Precision.HIGH, preferred_element_type=jnp.float32,
    )
    return (served.astype(jnp.float32) + delta).astype(jnp.bfloat16)


def solution(mesh):
    placed = (P("row", "col"), P("row", "col"), P("row", "col"))
    return jax.shard_map(
        body, mesh=mesh, in_specs=placed, out_specs=P(None, ("row", "col")), check_vma=False
    )
```

time: 2070 us -> 1240 us (0.60)
  blocking collectives: 1640 us -> 0 us
  Pallas kernels: 0 us -> 1190 us
  local copies, waits for them, and re-layouts: 164 us -> 0 us
  waiting for transfers between devices: 158 us -> 0 us
  matrix products: 90.8 us -> 51.4 us
    all_to_all x2 -> x0, blocking collectives: 1640 us -> none  [the longest x1 1090 us: to_serving(): lax.all_to_all(across, 'row', split_axis=1, concat_axis=0, tiled=True)]
    pallas_call x0 -> x1, Pallas kernels: none -> 1190 us  [move(): pl.pallas_call(functools.partial(transport, nr, nc), out_shape=[out((nr *...]
    all_gather x2 -> x0, waiting for transfers between devices: 156 us -> none  [the longest x1 119 us: body(): lax.all_gather(right_factor, 'row', axis=0, tiled=True)]
    reshape x2 -> x0, local copies, waits for them, and re-layouts: 131 us -> none  [to_serving(): shaped = stored.reshape(height, group_count, col_count, block_width)]
    dot_general x1, matrix products: 90.8 us -> 51.4 us  [body(): lax.dot_general(left_all, right_all, (((0,), (0,)), ((), ())), precision=...]
    unnamed x1 -> x0, local copies, waits for them, and re-layouts: 33.7 us -> none
  transfers between devices with their start and end apart: 2 -> 0, of which waited for: 2 -> 0; matrix products, arithmetic and copies ran while one was open for 0% -> 0% of each run, Pallas kernels for 0% -> 0%
where the time goes in v1:
time: 1240 us
  Pallas kernels  1190 us (96%)
  matrix products  51.4 us (4%)
    pallas_call x1, Pallas kernels, move(): pl.pallas_call(functools.partial(transport, nr, nc), out_shape=[out((nr *...  1190 us
    dot_general x1, matrix products, body(): lax.dot_general(left_all, right_all, (((0,), (0,)), ((), ())), precision=...  51.4 us

profile of v1, /device:TPU:5, one launch (start us, length us, event | category | flops | bytes accessed | tf_op | source)
XLA Modules:
  0.0 1242.0 jit_solution(17521994457959892194)
XLA Ops:
  0.0 1190.6 %shard_map.37 = (bf16[16384,1536]{1,0:T(8,128)(2,1)}, f32[256,16384]{1,0:T(8,128)}, f32[256,1536]{1,0:T(8,128)}, bf16[4,2,2048,1536]{3,2,1,0:T(8,128)(2,1)}, f32[4,2,32,1536]{3,2,1,0:T(8,128)}) custom-call(bf16[2048,12288]{1,0:T(8,128)(2,1)} %base.1, f32[64,2048]{1,0:T(8,128)} %bitcast.3, f32[32,12288]{1,0:T(8,128)} %right.1), custom_call_target="tpu_custom_call" | custom-call | tf_op jit(solution)/shard_map/pallas_call | solution.py:235
  1190.6 51.4 %add_convert_fusion = bf16[16384,1536]{1,0:T(8,128)(2,1)} fusion(bf16[16384,1536]{1,0:T(8,128)(2,1)} %get-tuple-element.8, f32[256,16384]{1,0:T(8,128)} %get-tuple-element.9, f32[256,1536]{1,0:T(8,128)} %get-tuple-element.10), kind=kOutput, calls=%fused_computation | convolution fusion | flops 38730203136 | bytes 119013376 | tf_op jit(solution)/shard_map/dot_general | solution.py:260

commit v2 on v1

--- a/solution.py
+++ b/solution.py
@@ -9,6 +9,7 @@
 
 CHUNKS = 8
 AHEAD = 2
+DELAY = 6
 MESH = pl.DeviceIdType.MESH
 
 
@@ -103,8 +104,8 @@
     own_small = own_sem.at[pl.ds(CHUNKS, 1)]
 
     def each_across(k, arrays, send, recv, act):
-        for g in range(ng):
-            for dj in range(1, nc):
+        for dj in range(1, nc):
+            for g in range(ng):
                 across(k, dj, g, *arrays, send, recv, act)
 
     def each_along(k, shifts, arrays, send, recv, own, act, act_own):
@@ -141,14 +142,9 @@
         pl.semaphore_signal(barrier, inc=1, device_id=(shifted(r, dq, nr), c), device_id_type=MESH)
     pl.semaphore_wait(barrier, nc + nr - 2)
 
-    def open_chunk(k):
-        each_across(k, big, a_send, a_recv, start)
-        each_along(k, (0,), big, b_send, b_recv, own_big, start, start)
-
     each_across(0, big, a_send, a_recv, start)
     for d in range(1, half):
         first_left(d).start()
-    each_along(0, (0,), big, b_send, b_recv, own_big, start, start)
     each_across(0, small, ra_send, ra_recv, start)
     each_along(0, (0,), small, rb_send, rb_recv, own_small, start, start)
     own_left = pltpu.make_async_copy(left, block(c, r), own_sem.at[CHUNKS + 1])
@@ -156,19 +152,29 @@
 
     @pl.loop(1, AHEAD)
     def _(k):
-        open_chunk(k)
+        each_across(k, big, a_send, a_recv, start)
+
+    plane = r // ng
+    at_end = jnp.logical_or(r < ng, r >= nr - ng)
 
     def forward(k):
-        for g in range(ng):
-            for ds in range(1, nc):
-                arrived(k, ds, g, *big, a_send, a_recv)
-        each_along(k, range(1, nc), big, b_send, b_recv, own_big, start, start)
-
-    @pl.loop(0, CHUNKS)
+        for ds in range(nc):
+            s = shifted(c, -ds, nc)
+            late = jnp.logical_and(at_end, jnp.abs(s - plane) >= 2)
+            turn = jnp.where(late, k - DELAY, k)
+
+            @pl.when(jnp.logical_and(turn >= 0, turn < CHUNKS))
+            def _():
+                for g in range(ng):
+                    if ds > 0:
+                        arrived(turn, ds, g, *big, a_send, a_recv)
+                    along(turn, ds, g, *big, b_send, b_recv, own_big, start, start)
+
+    @pl.loop(0, CHUNKS + DELAY)
     def _(k):
         @pl.when(k + AHEAD < CHUNKS)
         def _():
-            open_chunk(k + AHEAD)
+            each_across(k + AHEAD, big, a_send, a_recv, start)
 
         forward(k)
 

time: 1240 us -> 1220 us (0.984)
  Pallas kernels: 1190 us -> 1170 us
    pallas_call x1, Pallas kernels: 1190 us -> 1170 us  [move(): pl.pallas_call(functools.partial(transport, nr, nc), out_shape=[out((nr *...]
where the time goes in v2:
time: 1220 us
  Pallas kernels  1170 us (96%)
  matrix products  51.4 us (4%)
    pallas_call x1, Pallas kernels, move(): pl.pallas_call(functools.partial(transport, nr, nc), out_shape=[out((nr *...  1170 us
    dot_general x1, matrix products, body(): lax.dot_general(left_all, right_all, (((0,), (0,)), ((), ())), precision=...  51.4 us

profile of v2, /device:TPU:5, one launch (start us, length us, event | category | flops | bytes accessed | tf_op | source)
XLA Modules:
  0.0 1217.4 jit_solution(13730464840164307118)
XLA Ops:
  0.0 1166.0 %shard_map.37 = (bf16[16384,1536]{1,0:T(8,128)(2,1)}, f32[256,16384]{1,0:T(8,128)}, f32[256,1536]{1,0:T(8,128)}, bf16[4,2,2048,1536]{3,2,1,0:T(8,128)(2,1)}, f32[4,2,32,1536]{3,2,1,0:T(8,128)}) custom-call(bf16[2048,12288]{1,0:T(8,128)(2,1)} %base.1, f32[64,2048]{1,0:T(8,128)} %bitcast.3, f32[32,12288]{1,0:T(8,128)} %right.1), custom_call_target="tpu_custom_call" | custom-call | tf_op jit(solution)/shard_map/pallas_call | solution.py:241
  1166.0 51.4 %add_convert_fusion = bf16[16384,1536]{1,0:T(8,128)(2,1)} fusion(bf16[16384,1536]{1,0:T(8,128)(2,1)} %get-tuple-element.8, f32[256,16384]{1,0:T(8,128)} %get-tuple-element.9, f32[256,1536]{1,0:T(8,128)} %get-tuple-element.10), kind=kOutput, calls=%fused_computation | convolution fusion | flops 38730203136 | bytes 119013376 | tf_op jit(solution)/shard_map/dot_general | solution.py:266
